TPU v7x, 256 devices: a whole 4x4x8 slice. The times are simulated.
256 devices in a mesh: req: 32 (over y, x, core), tp: 8 (over z).
Axes of the slice: x: 4, y: 4, z: 8, core: 2. Of those that a mesh axis runs over, the one named last changes fastest.
Arguments:
- tokens: bfloat16 [32, 768, 2048], P('req', None, 'tp'), may hold values from -6 to 6
- q_weight: bfloat16 [2048, 2048], P(None, 'tp'), may hold values from -0.125 to 0.125
- k_weight: bfloat16 [2048, 2048], P(None, 'tp'), may hold values from -0.125 to 0.125
- v_weight: bfloat16 [2048, 2048], P(None, 'tp'), may hold values from -0.125 to 0.125
- o_weight: bfloat16 [2048, 2048], P('tp'), may hold values from -0.125 to 0.125
- q_gain: bfloat16 [2048], P('tp'), may hold values from 0.099609375 to 1.8984375
- k_gain: bfloat16 [2048], P('tp'), may hold values from 0.099609375 to 1.8984375
- post_gain: bfloat16 [2048], P('tp'), may hold values from 0.099609375 to 1.8984375
- key_pool: bfloat16 [1024, 128, 2048], P('req', None, 'tp'), may hold values from -400 to 400
- value_pool: bfloat16 [1024, 128, 2048], P('req', None, 'tp'), may hold values from -6 to 6
- cache_len: int32 [32], replicated, may hold values from 1 to 4096, as said below
- page_table: int32 [32, 32], replicated, may hold values from -1 to 1023, as said below
Outputs:
- mixed: bfloat16 [32, 768, 2048], P('req', None, 'tp')
- new_keys: bfloat16 [32, 768, 2048], P('req', None, 'tp')
- new_values: bfloat16 [32, 768, 2048], P('req', None, 'tp')
Inputs may be any that keep to these rules, and one draw needn't show every extreme that they name: `cache_len`: on some index of req the one request hold 4096 cached tokens. `page_table`: entry p of request r is a pool page (index d * 32 + local page of index d of req) for p < ceil(cache_len[r] / 128) and -1 otherwise; no pool page is named twice; the pages named by the requests of one index of req lie at most 1 on any one index of req, and some pair of indices reaches 1.
All inputs are finite; a program needn't handle non-finite values.
Results may differ from a plain program's by a relative error of at most 0.013.
Values may be sent and summed in bfloat16 or wider, within the bound.
No kernel may reach another device: no remote copies, remote signals or barrier semaphores. Data moves between devices by JAX's collectives and lax.ppermute only.
A program may use at most 64 MiB of HBM per device.

v0:
```python
import jax
import jax.numpy as jnp
from jax import lax
from jax.sharding import PartitionSpec as P

HEAD_DIM = 128
EPSILON = 1e-06
ROPE_BASE = 500000.0


def rotate(values, positions):
    half_dim = values.shape[-1] // 2
    freqs = jnp.power(
        jnp.float32(ROPE_BASE), -jnp.arange(half_dim, dtype=jnp.float32) * 2.0 / values.shape[-1]
    )
    angles = positions[..., None] * freqs
    cosine = jnp.cos(angles)[..., None, :]
    sine_part = jnp.sin(angles)[..., None, :]
    first_half = values[..., :half_dim]
    second_half = values[..., half_dim:]
    return jnp.concatenate(
        [
            first_half * cosine - second_half * sine_part,
            second_half * cosine + first_half * sine_part,
        ],
        -1,
    )


def page_slots(page_table, pool_dev):
    valid = page_table >= 0
    source = jnp.where(valid, page_table // pool_dev, -1)
    local = jnp.where(valid, page_table % pool_dev, 0)
    order = jnp.arange(page_table.shape[1])
    same = (
        (source[:, :, None] == source[:, None, :])
        & valid[:, None, :]
        & (order[None, :, None] > order[None, None, :])
    )
    rank = jnp.sum(same.astype(jnp.int32), -1)
    return (source, rank, valid, local)


def attend(query, cache_k, cache_v, fresh_k, fresh_v, lengths):
    scale = query.shape[-1] ** (-0.5)
    req_dev, block_len, heads_here, head_dim = query.shape
    cache_span = cache_k.shape[1]
    cache_mask = (jnp.arange(cache_span)[None, :] < lengths[:, None])[:, None, :]
    causal = (jnp.arange(block_len)[:, None] >= jnp.arange(block_len)[None, :])[None]

    def one_head(head):
        query_h = lax.dynamic_index_in_dim(query, head, 2, keepdims=False)
        cache_kh = lax.dynamic_index_in_dim(cache_k, head, 2, keepdims=False)
        cache_vh = lax.dynamic_index_in_dim(cache_v, head, 2, keepdims=False)
        fresh_kh = lax.dynamic_index_in_dim(fresh_k, head, 2, keepdims=False)
        fresh_vh = lax.dynamic_index_in_dim(fresh_v, head, 2, keepdims=False)
        cache_scores = (
            jnp.einsum("rqd,rkd->rqk", query_h, cache_kh, preferred_element_type=jnp.float32)
            * scale
        )
        fresh_scores = (
            jnp.einsum("rqd,rkd->rqk", query_h, fresh_kh, preferred_element_type=jnp.float32)
            * scale
        )
        scores = jnp.concatenate(
            [jnp.where(cache_mask, cache_scores, -1e30), jnp.where(causal, fresh_scores, -1e30)], -1
        )
        peak = jnp.max(scores, -1, keepdims=True)
        raised = jnp.exp(scores - peak)
        weights = (raised / jnp.sum(raised, -1, keepdims=True)).astype(jnp.bfloat16)
        result = jnp.einsum(
            "rqk,rkd->rqd", weights[..., :cache_span], cache_vh, preferred_element_type=jnp.float32
        )
        result = result + jnp.einsum(
            "rqk,rkd->rqd", weights[..., cache_span:], fresh_vh, preferred_element_type=jnp.float32
        )
        return result.astype(jnp.bfloat16)

    per_head = lax.map(one_head, jnp.arange(heads_here, dtype=jnp.int32))
    return jnp.transpose(per_head, (1, 2, 0, 3)).reshape(req_dev, block_len, heads_here * head_dim)


def body(
    tokens,
    q_weight,
    k_weight,
    v_weight,
    o_weight,
    q_gain,
    k_gain,
    post_gain,
    key_pool,
    value_pool,
    cache_len,
    page_table,
):
    req_dev, block_len, feature_part = tokens.shape
    model_width = q_weight.shape[0]
    columns = q_weight.shape[1]
    heads_here = columns // HEAD_DIM
    owners = lax.axis_size("req")
    owner = lax.axis_index("req")
    tensor_size = lax.axis_size("tp")
    row_count = req_dev * block_len
    flat = tokens.reshape(row_count, feature_part)
    empty = jnp.zeros((row_count, columns), jnp.float32)
    totals = (empty, empty, empty)
    piece = lax.all_gather(flat, "tp", axis=1, tiled=True)
    result = []
    for total, weight in zip(totals, (q_weight, k_weight, v_weight)):
        result.append(jnp.dot(piece, weight, preferred_element_type=jnp.float32))
    q_proj, k_proj, v_proj = tuple(result)
    q_squares, k_squares = lax.psum(
        (jnp.sum(q_proj * q_proj, 1), jnp.sum(k_proj * k_proj, 1)), "tp"
    )
    full_columns = columns * tensor_size
    q_normed = (
        q_proj * lax.rsqrt(q_squares / full_columns + EPSILON)[:, None] * q_gain.astype(jnp.float32)
    )
    k_normed = (
        k_proj * lax.rsqrt(k_squares / full_columns + EPSILON)[:, None] * k_gain.astype(jnp.float32)
    )
    lengths = lax.dynamic_slice_in_dim(cache_len, owner * req_dev, req_dev)
    positions = (lengths[:, None] + jnp.arange(block_len, dtype=jnp.int32)[None, :]).astype(
        jnp.float32
    )
    query = rotate(q_normed.reshape(req_dev, block_len, heads_here, HEAD_DIM), positions).astype(
        jnp.bfloat16
    )
    new_keys = rotate(k_normed.reshape(req_dev, block_len, heads_here, HEAD_DIM), positions).astype(
        jnp.bfloat16
    )
    new_values = v_proj.astype(jnp.bfloat16).reshape(req_dev, block_len, heads_here, HEAD_DIM)
    pool_dev = key_pool.shape[0]
    page_len = key_pool.shape[1]
    pair_cap = pool_dev // owners
    source, rank, valid, local = page_slots(page_table, pool_dev)
    match = (
        valid[:, None, :]
        & (source[:, None, :] == owner)
        & (rank[:, None, :] == jnp.arange(pair_cap)[None, :, None])
    )
    chosen = jnp.sum(jnp.where(match, local[:, None, :], 0), -1).reshape(-1)
    outgoing_k = key_pool[chosen]
    outgoing_v = value_pool[chosen]
    arrived_k, arrived_v = (
        lax.all_to_all(outgoing_k, "req", split_axis=0, concat_axis=0, tiled=True),
        lax.all_to_all(outgoing_v, "req", split_axis=0, concat_axis=0, tiled=True),
    )
    mine_source = lax.dynamic_index_in_dim(source, owner, 0, keepdims=False)
    mine_rank = lax.dynamic_index_in_dim(rank, owner, 0, keepdims=False)
    mine_valid = lax.dynamic_index_in_dim(valid, owner, 0, keepdims=False)
    placement = jnp.where(mine_valid, mine_source * pair_cap + mine_rank, 0)
    cache_span = page_table.shape[1] * page_len
    cache_k = arrived_k[placement].reshape(req_dev, cache_span, heads_here, HEAD_DIM)
    cache_v = arrived_v[placement].reshape(req_dev, cache_span, heads_here, HEAD_DIM)
    attended = attend(query, cache_k, cache_v, new_keys, new_values, lengths)
    partial_value = jnp.dot(
        attended.reshape(row_count, columns), o_weight, preferred_element_type=jnp.float32
    )
    summed = lax.psum(partial_value.astype(jnp.bfloat16), "tp").astype(jnp.float32)
    squares = jnp.sum(summed * summed, 1)
    normed_all = summed * lax.rsqrt(squares / model_width + EPSILON)[:, None]
    normed = lax.dynamic_slice_in_dim(
        normed_all, lax.axis_index("tp") * feature_part, feature_part, 1
    )
    mixed = (flat.astype(jnp.float32) + normed * post_gain.astype(jnp.float32)).astype(jnp.bfloat16)
    return (
        mixed.reshape(req_dev, block_len, feature_part),
        new_keys.reshape(req_dev, block_len, columns),
        new_values.reshape(req_dev, block_len, columns),
    )


def solution(mesh):
    placed = (
        P("req", None, "tp"),
        P(None, "tp"),
        P(None, "tp"),
        P(None, "tp"),
        P("tp", None),
        P("tp"),
        P("tp"),
        P("tp"),
        P("req", None, "tp"),
        P("req", None, "tp"),
        P(),
        P(),
    )
    return jax.shard_map(
        body,
        mesh=mesh,
        in_specs=placed,
        out_specs=(P("req", None, "tp"), P("req", None, "tp"), P("req", None, "tp")),
        check_vma=False,
    )
```

profile of v0, /device:TPU:1, one launch (start us, length us, event | category | flops | bytes accessed | tf_op | source)
XLA Modules:
  0.0 275.5 jit_solution(12910835094052155758)
XLA Ops:
  7.2 0.7 all-gather.3.cloned.1.call-update
  7.9 0.7 iota_compare_fusion.1
  8.6 0.7 fusion.45
  9.4 0.8 convert_reduce_fusion
  10.2 0.9 fusion.48
  11.1 2.0 gather_fusion
  13.1 8.6 %all-to-all-start = ((bf16[32,128,256]{2,1,0:T(8,128)(2,1)}), bf16[32,128,256]{2,1,0:T(8,128)(2,1)S(1)}, u32[]{:S(2)}, u32[]{:S(2)}) async-start(bf16[32,128,256]{2,1,0:T(8,128)(2,1)} %gather_fusion), calls=%async_computation | async-start | bytes 4194304 | tf_op jit(solution)/shard_map/all_to_all | solution.py:147
  21.7 3.6 %gather_fusion.2 = bf16[32,128,256]{2,1,0:T(8,128)(2,1)} fusion(bf16[32,128,256]{2,1,0:T(8,128)(2,1)} %param.23, s32[1024]{0:T(1024)S(1)} %pad_clamp_fusion.1), kind=kCustom, calls=%fused_computation.2 | custom fusion | bytes 4194432 | tf_op jit(solution)/shard_map/gather | solution.py:145
  25.3 25.0 %all-to-all-done = bf16[32,128,256]{2,1,0:T(8,128)(2,1)S(1)} async-done(((bf16[32,128,256]{2,1,0:T(8,128)(2,1)}), bf16[32,128,256]{2,1,0:T(8,128)(2,1)S(1)}, u32[]{:S(2)}, u32[]{:S(2)}) %all-to-all-start) | async-done | bytes 2097184 | tf_op jit(solution)/shard_map/all_to_all | solution.py:147
  50.3 6.0 %all-to-all-start.1 = ((bf16[32,128,256]{2,1,0:T(8,128)(2,1)}), bf16[32,128,256]{2,1,0:T(8,128)(2,1)}, u32[]{:S(2)}, u32[]{:S(2)}) async-start(bf16[32,128,256]{2,1,0:T(8,128)(2,1)} %gather_fusion.2), calls=%async_computation.1 | async-start | bytes 4194304 | tf_op jit(solution)/shard_map/all_to_all | solution.py:148
  56.4 0.6 dynamic_slice.38
  57.0 0.6 add_convert_fusion.1
  57.6 1.4 multiply_cosine_fusion
  59.1 2.1 gather_fusion.1
  61.1 3.9 %reshape.515 = bf16[1,4096,2,128]{3,2,1,0:T(2,128)(2,1)} reshape(bf16[32,128,256]{2,1,0:T(8,128)(2,1)} %gather_fusion.1) | data formatting | bytes 4194304 | tf_op jit(solution)/shard_map/reshape | solution.py:155
  65.1 1.9 copy.51
  66.9 17.7 %all-to-all-done.1 = bf16[32,128,256]{2,1,0:T(8,128)(2,1)} async-done(((bf16[32,128,256]{2,1,0:T(8,128)(2,1)}), bf16[32,128,256]{2,1,0:T(8,128)(2,1)}, u32[]{:S(2)}, u32[]{:S(2)}) %all-to-all-start.1) | async-done | bytes 2097184 | tf_op jit(solution)/shard_map/all_to_all | solution.py:148
  84.7 3.6 %gather_fusion.3 = bf16[32,128,256]{2,1,0:T(8,128)(2,1)} fusion(bf16[32,128,256]{2,1,0:T(8,128)(2,1)} %all-to-all-done.1, s32[1024]{0:T(1024)S(1)} %pad_clamp_fusion), kind=kCustom, calls=%fused_computation.3 | custom fusion | bytes 4194432 | tf_op jit(solution)/shard_map/gather | solution.py:156
  88.3 4.0 %reshape.516 = bf16[1,4096,2,128]{3,2,1,0:T(2,128)(2,1)} reshape(bf16[32,128,256]{2,1,0:T(8,128)(2,1)} %gather_fusion.3) | data formatting | bytes 4194304 | tf_op jit(solution)/shard_map/reshape | solution.py:156
  92.3 3.2 %copy.52 = bf16[1,4096,2,128]{3,1,2,0:T(8,128)(2,1)} copy(bf16[1,4096,2,128]{3,2,1,0:T(2,128)(2,1)} %reshape.516) | data formatting | bytes 4194304
  95.5 4.3 %multiply_reduce_fusion.2 = (f32[768]{0:T(1024)S(1)}, f32[768,256]{0,1:T(8,128)}) fusion(bf16[2048,256]{1,0:T(8,128)(2,1)} %param.15, bf16[1,768,2048]{2,1,0:T(8,128)(2,1)} %all-gather.3.cloned.1.call-done), kind=kOutput, calls=%fused_computation.65 | convolution fusion | flops 805698816 | bytes 4983808 | tf_op jit(solution)/shard_map/dot_general | solution.py:111
  99.7 2.0 multiply_reduce_fusion.1
  101.7 16.7 %all-reduce = (f32[768]{0:T(1024)S(1)}, f32[768]{0:T(1024)S(1)}) all-reduce(f32[768]{0:T(1024)S(1)} %get-tuple-element.160, f32[768]{0:T(1024)S(1)} %get-tuple-element.162), channel_id=1, replica_groups=mesh['req'=32,'tp'=8] {'tp'}, use_global_device_ids=true, to_apply=%region_1.0 | all-reduce | flops 1536 | bytes 12288 | tf_op jit(solution)/shard_map/psum | solution.py:113
  118.4 1.3 multiply_multiply_fusion
  119.7 0.8 fusion.54
  120.5 2.2 copy.67
  122.7 1.2 copy.68
  123.8 1.3 multiply_multiply_fusion.1
  125.1 0.8 fusion.55
  125.9 2.2 copy.65
  128.1 1.2 copy.66
  129.3 1.7 multiply_subtract_fusion
  131.0 1.0 maximum_convert_fusion
  132.4 0.8 copy-done.12
  133.2 0.3 copy-done.14
  133.5 1.8 fusion.38
  135.3 34.6 %while.11 = (s32[]{:T(128)}, bf16[2,1,768,128]{2,3,0,1:T(8,128)(2,1)}, s32[2]{0:T(128)S(1)}, bf16[1,768,2,128]{3,1,2,0:T(8,128)(2,1)S(1)}, bf16[1,4096,2,128]{3,...) while((s32[]{:T(128)}, ...), condition=%wide.region_10.11_spmd.clone, body=%wide.region_6.10_spmd.clone.sunk | while | flops 1950747136 | bytes 74421992 | solution.py:79
  135.3 0.6 dynamic_slice.119
  137.6 0.6 compare_reduce_fusion.2
  138.2 2.2 fusion.89
  140.4 1.5 fusion.88
  141.9 4.4 %fusion.90 = f32[768]{0:T(1024)S(1)} fusion(f32[1,768,768]{2,1,0:T(8,128)S(1)} %get-tuple-element.227, f32[1,768,4096]{2,1,0:T(8,128)S(1)} %get-tuple-element.228, f32[768]{0:T(1024)S(1)} %reduce_max.30), kind=kLoop, calls=%fused_computation.12.clone.1 | loop fusion | flops 11205888 | bytes 14948352 | tf_op jit(solution)/shard_map/while/body/eval_jaxpr/reduce_sum | solution.py:70
  146.3 3.1 %divide_convert_fusion.2 = bf16[1,768,4864]{2,1,0:T(8,128)(2,1)S(1)} fusion(f32[1,768,768]{2,1,0:T(8,128)S(1)} %get-tuple-element.227, f32[1,768,4096]{2,1,0:T(8,128)S(1)} %get-tuple-element.228, f32[768]{0:T(1024)S(1)} %fusion.90, f32[768]{0:T(1024)S(1)} %reduce_max.30), kind=kLoop, calls=%fused_computation.8.clone.1 | loop fusion | flops 14942208 | bytes 22419456 | tf_op jit(solution)/shard_map/while/body/eval_jaxpr/convert_element_type | solution.py:70
  149.5 1.8 fusion.91
  151.3 0.5 fusion.92
  151.9 0.7 constant_dynamic-update-slice_fusion.2
  152.6 0.6 dynamic_slice.119
  154.9 0.6 compare_reduce_fusion.2
  155.5 2.2 fusion.89
  157.7 1.5 fusion.88
  159.2 4.4 %fusion.90 = f32[768]{0:T(1024)S(1)} fusion(f32[1,768,768]{2,1,0:T(8,128)S(1)} %get-tuple-element.227, f32[1,768,4096]{2,1,0:T(8,128)S(1)} %get-tuple-element.228, f32[768]{0:T(1024)S(1)} %reduce_max.30), kind=kLoop, calls=%fused_computation.12.clone.1 | loop fusion | flops 11205888 | bytes 14948352 | tf_op jit(solution)/shard_map/while/body/eval_jaxpr/reduce_sum | solution.py:70
  163.6 3.1 %divide_convert_fusion.2 = bf16[1,768,4864]{2,1,0:T(8,128)(2,1)S(1)} fusion(f32[1,768,768]{2,1,0:T(8,128)S(1)} %get-tuple-element.227, f32[1,768,4096]{2,1,0:T(8,128)S(1)} %get-tuple-element.228, f32[768]{0:T(1024)S(1)} %fusion.90, f32[768]{0:T(1024)S(1)} %reduce_max.30), kind=kLoop, calls=%fused_computation.8.clone.1 | loop fusion | flops 14942208 | bytes 22419456 | tf_op jit(solution)/shard_map/while/body/eval_jaxpr/convert_element_type | solution.py:70
  166.8 1.8 fusion.91
  168.6 0.5 fusion.92
  169.2 0.7 constant_dynamic-update-slice_fusion.2
  169.9 4.0 %convolution_convert_fusion = bf16[768,2048]{1,0:T(8,128)(2,1)} fusion(bf16[768,256]{0,1:T(8,128)(2,1)} %bitcast.119, bf16[256,2048]{1,0:T(8,128)(2,1)} %param.18), kind=kOutput, calls=%fused_computation.45 | convolution fusion | flops 806879232 | bytes 4587520 | tf_op jit(solution)/shard_map/dot_general | solution.py:158
  174.0 0.6 copy-done.18
  174.6 0.4 copy-done.10
  175.0 0.9 copy.56
  175.9 1.0 copy_bitcast_fusion
  176.8 87.0 %all-reduce.3.cloned.1.call-done = bf16[768,2048]{1,0:T(8,128)(2,1)} async-done(((bf16[768,2048]{1,0:T(8,128)(2,1)}), bf16[768,2048]{1,0:T(8,128)(2,1)}) %all-reduce.3.cloned.1.call-update) | async-done | bytes 3145744 | tf_op jit(solution)/shard_map/psum | solution.py:161
  263.8 2.7 multiply_reduce_fusion
  266.7 0.8 convert_element_type.89
  267.7 0.9 fusion.44
  (60 shorter events, 1.2 us)
Async XLA Ops:
  7.2 3.9 %copy-start = (bf16[32,128,256]{2,1,0:T(8,128)(2,1)S(1)}, bf16[32,128,256]{2,1,0:T(8,128)(2,1)}, u32[]{:S(2)}) copy-start(bf16[32,128,256]{2,1,0:T(8,128)(2,1)} %param.22) | copy-start | bytes 6291460
  7.2 88.3 %all-gather.3.cloned.1.call-start = ((), (), s32[]{:S(2)}) async-start(), calls=%async_computation.3 | async-start | bytes 3538944 | tf_op jit(solution)/shard_map/all_gather | solution.py:108
  13.1 37.2 %all-to-all-start = ((bf16[32,128,256]{2,1,0:T(8,128)(2,1)}), bf16[32,128,256]{2,1,0:T(8,128)(2,1)S(1)}, u32[]{:S(2)}, u32[]{:S(2)}) async-start(bf16[32,128,256]{2,1,0:T(8,128)(2,1)} %gather_fusion), calls=%async_computation | async-start | bytes 4194304 | tf_op jit(solution)/shard_map/all_to_all | solution.py:147
  25.3 31.1 %copy-start.15 = (bf16[256]{0:T(256)(128)(2,1)S(1)}, bf16[256]{0:T(256)(128)(2,1)}, u32[]{:S(2)}) copy-start(bf16[256]{0:T(256)(128)(2,1)} %param.20) | copy-start | bytes 1540
  25.3 31.1 %copy-start.16 = (bf16[256]{0:T(256)(128)(2,1)S(1)}, bf16[256]{0:T(256)(128)(2,1)}, u32[]{:S(2)}) copy-start(bf16[256]{0:T(256)(128)(2,1)} %param.19) | copy-start | bytes 1540
  25.3 31.1 %copy-start.17 = (s32[32]{0:T(128)S(1)}, s32[32]{0:T(128)}, u32[]{:S(2)}) copy-start(s32[32]{0:T(128)} %param.24) | copy-start | bytes 388
  50.3 34.4 %all-to-all-start.1 = ((bf16[32,128,256]{2,1,0:T(8,128)(2,1)}), bf16[32,128,256]{2,1,0:T(8,128)(2,1)}, u32[]{:S(2)}, u32[]{:S(2)}) async-start(bf16[32,128,256]{2,1,0:T(8,128)(2,1)} %gather_fusion.2), calls=%async_computation.1 | async-start | bytes 4194304 | tf_op jit(solution)/shard_map/all_to_all | solution.py:148
  56.3 207.5 %all-reduce.3.cloned.1.call-start = ((), (), s32[]{:S(2)}) async-start(), calls=%async_computation.2 | async-start | bytes 6291456 | tf_op jit(solution)/shard_map/psum | solution.py:161
  95.5 4.3 %copy-start.11 = (bf16[1,768,2048]{2,1,0:T(8,128)(2,1)S(1)}, bf16[1,768,2048]{2,1,0:T(8,128)(2,1)}, u32[]{:S(2)}) copy-start(bf16[1,768,2048]{2,1,0:T(8,128)(2,1)} %all-gather.3.cloned.1.call-done) | copy-start | bytes 9437188
  95.5 4.3 %copy-start.13 = (bf16[2048,256]{1,0:T(8,128)(2,1)S(1)}, bf16[2048,256]{1,0:T(8,128)(2,1)}, u32[]{:S(2)}) copy-start(bf16[2048,256]{1,0:T(8,128)(2,1)} %param.16) | copy-start | bytes 3145732
  129.3 2.7 copy-start.5
  129.3 2.7 copy-start.6
  131.0 1.2 copy-start.3
  131.0 2.2 copy-start.12
  131.0 2.5 copy-start.14
  146.3 3.2 %copy-start.7 = (bf16[1,4096,2,128]{3,1,2,0:T(8,128)(2,1)S(1)}, bf16[1,4096,2,128]{3,1,2,0:T(8,128)(2,1)}, u32[]{:S(2)}) copy-start(bf16[1,4096,2,128]{3,1,2,0:T(8,128)(2,1)} %get-tuple-element.261) | copy-start | bytes 6291460 | tf_op jit(solution)/shard_map/while
  149.5 1.8 copy-start.9
  163.6 3.2 %copy-start.7 = (bf16[1,4096,2,128]{3,1,2,0:T(8,128)(2,1)S(1)}, bf16[1,4096,2,128]{3,1,2,0:T(8,128)(2,1)}, u32[]{:S(2)}) copy-start(bf16[1,4096,2,128]{3,1,2,0:T(8,128)(2,1)} %get-tuple-element.261) | copy-start | bytes 6291460 | tf_op jit(solution)/shard_map/while
  166.8 1.8 copy-start.9
  174.0 0.7 copy-start.18
  174.0 1.0 copy-start.10
  174.0 1.9 copy-start.4
  263.8 2.8 %copy-start.2 = (bf16[768,2048]{1,0:T(8,128)(2,1)S(1)}, bf16[768,2048]{1,0:T(8,128)(2,1)}, u32[]{:S(2)}) copy-start(bf16[768,2048]{1,0:T(8,128)(2,1)} %all-reduce.3.cloned.1.call-done) | copy-start | bytes 9437188
  266.7 1.0 copy-start.8
  266.7 1.9 copy-start.1
Sparse Core Ops, SparseCore 0:
  9.7 54.7 all-gather.2
  174.1 89.6 all-reduce.2
where the time goes:
time: 276 us; the launch traced here: 275 us
  waiting for transfers between devices  130 us (47%)
  local copies, waits for them, and re-layouts  39.3 us (14%)
  other arithmetic  32.5 us (12%)
  matrix products  24 us (9%)
  blocking collectives  16.7 us (6%)
  starting transfers between devices  14.7 us (5%)
  between operations  14.3 us (5%)
  loops' own time  3.58 us (1%)
    psum x1, waiting for transfers between devices, body(): lax.psum(partial_value.astype(jnp.bfloat16), 'tp').astype(jnp.float32)  87 us
    all_to_all x1, waiting for transfers between devices, body(): lax.all_to_all(outgoing_k, 'req', split_axis=0, concat_axis=0, tiled=True)  25 us
    all_to_all x1, waiting for transfers between devices, body(): lax.all_to_all(outgoing_v, 'req', split_axis=0, concat_axis=0, tiled=True)  17.7 us
    psum x1, blocking collectives, body(): lax.psum((jnp.sum(q_proj * q_proj, 1), jnp.sum(k_proj * k_proj, 1)), 'tp')  16.7 us
    unnamed x41, local copies, waits for them, and re-layouts  15 us
    reduce_sum x2, other arithmetic, one_head(): weights = (raised / jnp.sum(raised, -1, keepdims=True)).astype(jnp.bfloat16)  8.73 us
    all_to_all x1, starting transfers between devices, body(): lax.all_to_all(outgoing_k, 'req', split_axis=0, concat_axis=0, tiled=True)  8.58 us
    dot_general x3, matrix products, body(): result.append(jnp.dot(piece, weight, preferred_element_type=jnp.float32))  8.09 us
  transfers between devices with their start and end apart: 4, of which 3 were waited for; matrix products, arithmetic and copies ran while one was open for 12% of the time, Pallas kernels for 0%

commit v1 on v0

--- a/solution.py
+++ b/solution.py
@@ -158,7 +158,9 @@
     partial_value = jnp.dot(
         attended.reshape(row_count, columns), o_weight, preferred_element_type=jnp.float32
     )
-    summed = lax.psum(partial_value.astype(jnp.bfloat16), "tp").astype(jnp.float32)
+    summed = jnp.sum(lax.all_gather(partial_value.astype(jnp.bfloat16), "tp"), axis=0).astype(
+        jnp.float32
+    )
     squares = jnp.sum(summed * summed, 1)
     normed_all = summed * lax.rsqrt(squares / model_width + EPSILON)[:, None]
     normed = lax.dynamic_slice_in_dim(

time: 276 us -> 448 us (1.62)
  waiting for transfers between devices: 130 us -> 292 us
  other arithmetic: 32.5 us -> 47.1 us
  local copies, waits for them, and re-layouts: 39.3 us -> 34.3 us
    all_gather x0 -> x1, waiting for transfers between devices: none -> 247 us  [body(): lax.all_gather(partial_value.astype(jnp.bfloat16), 'tp')]
    psum x1 -> x0, waiting for transfers between devices: 87 us -> none  [body(): lax.psum(partial_value.astype(jnp.bfloat16), 'tp').astype(jnp.float32)]
    reduce_sum x0 -> x1, other arithmetic: none -> 15.7 us  [body(): jnp.sum(lax.all_gather(partial_value.astype(jnp.bfloat16), 'tp'), axis=0)]
    all_to_all x1, waiting for transfers between devices: 17.7 us -> 25 us  [body(): lax.all_to_all(outgoing_v, 'req', split_axis=0, concat_axis=0, tiled=True)]
    all_to_all x1, waiting for transfers between devices: 25 us -> 19.4 us  [body(): lax.all_to_all(outgoing_k, 'req', split_axis=0, concat_axis=0, tiled=True)]
    unnamed x41 -> x43, local copies, waits for them, and re-layouts: 15 us -> 14.4 us
  transfers between devices with their start and end apart: 4 -> 4, of which waited for: 3 -> 3; matrix products, arithmetic and copies ran while one was open for 12% -> 6% of each run, Pallas kernels for 0% -> 0%
where the time goes in v1:
time: 448 us; the launch traced here: 447 us
  waiting for transfers between devices  292 us (65%)
  other arithmetic  47.1 us (11%)
  local copies, waits for them, and re-layouts  34.3 us (8%)
  matrix products  24.1 us (5%)
  blocking collectives  16.5 us (4%)
  starting transfers between devices  14.7 us (3%)
  between operations  14.3 us (3%)
    all_gather x1, waiting for transfers between devices, body(): lax.all_gather(partial_value.astype(jnp.bfloat16), 'tp')  247 us
    all_to_all x1, waiting for transfers between devices, body(): lax.all_to_all(outgoing_v, 'req', split_axis=0, concat_axis=0, tiled=True)  25 us
    all_to_all x1, waiting for transfers between devices, body(): lax.all_to_all(outgoing_k, 'req', split_axis=0, concat_axis=0, tiled=True)  19.4 us
    psum x1, blocking collectives, body(): lax.psum((jnp.sum(q_proj * q_proj, 1), jnp.sum(k_proj * k_proj, 1)), 'tp')  16.5 us
    reduce_sum x1, other arithmetic, body(): jnp.sum(lax.all_gather(partial_value.astype(jnp.bfloat16), 'tp'), axis=0)  15.7 us
    unnamed x43, local copies, waits for them, and re-layouts  14.4 us
  transfers between devices with their start and end apart: 4, of which 3 were waited for; matrix products, arithmetic and copies ran while one was open for 6% of the time, Pallas kernels for 0%

profile of v1, /device:TPU:1, one launch (start us, length us, event | category | flops | bytes accessed | tf_op | source)
XLA Modules:
  0.0 447.1 jit_solution(12921070034811374400)
XLA Ops:
  7.2 0.7 all-gather.5.cloned.1.call-update
  7.9 0.7 iota_compare_fusion.1
  8.6 0.7 fusion.45
  9.4 0.8 convert_reduce_fusion
  10.2 0.9 fusion.48
  11.1 2.0 gather_fusion.2
  13.1 8.6 %all-to-all-start.1 = ((bf16[32,128,256]{2,1,0:T(8,128)(2,1)}), bf16[32,128,256]{2,1,0:T(8,128)(2,1)S(1)}, u32[]{:S(2)}, u32[]{:S(2)}) async-start(bf16[32,128,256]{2,1,0:T(8,128)(2,1)} %gather_fusion.2), calls=%async_computation.1 | async-start | bytes 4194304 | tf_op jit(solution)/shard_map/all_to_all | solution.py:148
  21.7 3.6 gather_fusion
  25.3 25.0 %all-to-all-done.1 = bf16[32,128,256]{2,1,0:T(8,128)(2,1)S(1)} async-done(((bf16[32,128,256]{2,1,0:T(8,128)(2,1)}), bf16[32,128,256]{2,1,0:T(8,128)(2,1)S(1)}, u32[]{:S(2)}, u32[]{:S(2)}) %all-to-all-start.1) | async-done | bytes 2097184 | tf_op jit(solution)/shard_map/all_to_all | solution.py:148
  50.2 6.1 %all-to-all-start = ((bf16[32,128,256]{2,1,0:T(8,128)(2,1)}), bf16[32,128,256]{2,1,0:T(8,128)(2,1)}, u32[]{:S(2)}, u32[]{:S(2)}) async-start(bf16[32,128,256]{2,1,0:T(8,128)(2,1)} %gather_fusion), calls=%async_computation | async-start | bytes 4194304 | tf_op jit(solution)/shard_map/all_to_all | solution.py:147
  56.4 0.6 dynamic_slice.38
  57.0 0.6 add_convert_fusion.1
  57.6 1.4 multiply_cosine_fusion
  59.0 2.0 gather_fusion.3
  61.1 2.5 reshape.517
  63.6 1.6 copy.52
  65.2 19.4 %all-to-all-done = bf16[32,128,256]{2,1,0:T(8,128)(2,1)} async-done(((bf16[32,128,256]{2,1,0:T(8,128)(2,1)}), bf16[32,128,256]{2,1,0:T(8,128)(2,1)}, u32[]{:S(2)}, u32[]{:S(2)}) %all-to-all-start) | async-done | bytes 2097184 | tf_op jit(solution)/shard_map/all_to_all | solution.py:147
  84.7 2.3 gather_fusion.1
  87.0 2.1 reshape.516
  89.1 1.9 copy.51
  91.0 4.3 multiply_reduce_fusion.1
  95.2 2.0 multiply_reduce_fusion.2
  97.2 16.5 %all-reduce = (f32[768]{0:T(1024)S(1)}, f32[768]{0:T(1024)S(1)}) all-reduce(f32[768]{0:T(1024)S(1)} %get-tuple-element.160, f32[768]{0:T(1024)S(1)} %get-tuple-element.162), channel_id=1, replica_groups=mesh['req'=32,'tp'=8] {'tp'}, use_global_device_ids=true, to_apply=%region_1.0 | all-reduce | flops 1536 | bytes 12288 | tf_op jit(solution)/shard_map/psum | solution.py:113
  113.7 1.3 multiply_multiply_fusion.1
  115.1 0.8 fusion.55
  116.0 1.0 fusion.54
  117.0 2.1 copy.68
  119.1 2.2 copy.66
  121.3 2.2 copy.67
  123.5 1.2 copy.65
  124.7 1.7 multiply_subtract_fusion
  126.4 1.0 maximum_convert_fusion
  127.8 0.8 copy-done.13
  128.6 0.3 copy-done.15
  128.9 1.8 fusion.38
  130.7 35.0 %while.11 = (s32[]{:T(128)}, bf16[2,1,768,128]{2,3,0,1:T(8,128)(2,1)}, s32[2]{0:T(128)S(1)}, bf16[1,768,2,128]{3,1,2,0:T(8,128)(2,1)S(1)}, bf16[1,4096,2,128]{3,...) while((s32[]{:T(128)}, ...), condition=%wide.region_10.11_spmd.clone, body=%wide.region_6.10_spmd.clone.sunk | while | flops 1950747136 | bytes 74421496 | solution.py:79
  130.7 0.6 dynamic_slice.119
  133.2 0.6 compare_reduce_fusion.2
  133.8 1.5 fusion.88
  135.3 2.2 fusion.89
  137.5 4.4 fusion.90
  141.9 3.1 divide_convert_fusion.2
  145.1 1.8 fusion.91
  146.9 0.5 fusion.92
  147.5 0.7 constant_dynamic-update-slice_fusion.2
  148.2 0.6 dynamic_slice.119
  150.7 0.6 compare_reduce_fusion.2
  151.4 1.5 fusion.88
  152.8 2.2 fusion.89
  155.0 4.4 fusion.90
  159.4 3.1 divide_convert_fusion.2
  162.6 1.8 fusion.91
  164.4 0.5 fusion.92
  165.0 0.7 constant_dynamic-update-slice_fusion.2
  165.7 4.1 convolution_convert_fusion
  169.8 0.6 copy-done.19
  170.5 0.4 copy-done.11
  170.8 0.9 copy.56
  171.7 1.0 copy_bitcast_fusion
  172.7 247.1 %all-gather.7.cloned.1.call-done = bf16[6144,2048]{1,0:T(8,128)(2,1)} async-done(((bf16[768,2048]{1,0:T(8,128)(2,1)}), bf16[6144,2048]{1,0:T(8,128)(2,1)}) %all-gather.7.cloned.1.call-update) | async-done | bytes 25165840 | tf_op jit(solution)/shard_map/all_gather | solution.py:161
  419.8 15.7 %reduce_sum.73 = bf16[768,2048]{1,0:T(8,128)(2,1)} reduce(bf16[8,768,2048]{2,1,0:T(8,128)(2,1)} %bitcast.118, bf16[]{:T(256)} %constant.91.clone.1), dimensions={0}, to_apply=%region_11.12 | reduce | flops 11010048 | bytes 28311554 | tf_op jit(solution)/shard_map/reduce_sum | solution.py:161
  435.4 2.7 multiply_reduce_fusion
  438.3 0.8 convert_element_type.91
  439.3 0.9 fusion.44
  (63 shorter events, 1.4 us)
Async XLA Ops:
  7.2 3.9 copy-start
  7.2 83.8 %all-gather.5.cloned.1.call-start = ((), (), s32[]{:S(2)}) async-start(), calls=%async_computation.2 | async-start | bytes 3538944 | tf_op jit(solution)/shard_map/all_gather | solution.py:108
  13.1 37.2 %all-to-all-start.1 = ((bf16[32,128,256]{2,1,0:T(8,128)(2,1)}), bf16[32,128,256]{2,1,0:T(8,128)(2,1)S(1)}, u32[]{:S(2)}, u32[]{:S(2)}) async-start(bf16[32,128,256]{2,1,0:T(8,128)(2,1)} %gather_fusion.2), calls=%async_computation.1 | async-start | bytes 4194304 | tf_op jit(solution)/shard_map/all_to_all | solution.py:148
  25.3 31.1 %copy-start.16 = (bf16[256]{0:T(256)(128)(2,1)S(1)}, bf16[256]{0:T(256)(128)(2,1)}, u32[]{:S(2)}) copy-start(bf16[256]{0:T(256)(128)(2,1)} %param.19) | copy-start | bytes 1540
  25.3 31.1 %copy-start.17 = (bf16[256]{0:T(256)(128)(2,1)S(1)}, bf16[256]{0:T(256)(128)(2,1)}, u32[]{:S(2)}) copy-start(bf16[256]{0:T(256)(128)(2,1)} %param.20) | copy-start | bytes 1540
  25.3 31.1 %copy-start.18 = (s32[32]{0:T(128)S(1)}, s32[32]{0:T(128)}, u32[]{:S(2)}) copy-start(s32[32]{0:T(128)} %param.24) | copy-start | bytes 388
  50.2 34.4 %all-to-all-start = ((bf16[32,128,256]{2,1,0:T(8,128)(2,1)}), bf16[32,128,256]{2,1,0:T(8,128)(2,1)}, u32[]{:S(2)}, u32[]{:S(2)}) async-start(bf16[32,128,256]{2,1,0:T(8,128)(2,1)} %gather_fusion), calls=%async_computation | async-start | bytes 4194304 | tf_op jit(solution)/shard_map/all_to_all | solution.py:147
  56.3 363.5 %all-gather.7.cloned.1.call-start = ((), (), s32[]{:S(2)}) async-start(), calls=%async_computation.3 | async-start | bytes 28311552 | tf_op jit(solution)/shard_map/all_gather | solution.py:161
  90.9 4.3 copy-start.12
  91.0 4.3 copy-start.14
  113.7 2.2 copy-start.9
  124.7 2.7 copy-start.5
  124.7 2.7 copy-start.6
  126.4 1.2 copy-start.3
  126.4 2.2 copy-start.13
  126.4 2.5 copy-start.15
  141.9 3.2 copy-start.7
  145.1 1.8 copy-start.10
  159.4 3.2 copy-start.7
  162.6 1.8 copy-start.10
  169.8 0.7 copy-start.19
  169.8 1.0 copy-start.11
  169.8 1.9 copy-start.4
  435.4 2.8 copy-start.2
  438.3 1.0 copy-start.8
  438.3 1.9 copy-start.1
Sparse Core Ops, SparseCore 0:
  9.7 54.7 all-gather.4
  170.0 249.7 all-gather.6
